TPU v7x, 32 devices: a whole 2x2x4 slice. The times are simulated.
32 devices in a mesh: groups: 2 (over y), tile: 8 (over z, x), col: 2 (over core).
Axes of the slice: x: 2, y: 2, z: 4, core: 2. Of those that a mesh axis runs over, the one named last changes fastest.
Arguments:
- jacobian: bfloat16 [512, 3, 128, 512], P(('groups', 'tile'), None, None, 'col'), parts along dimension 0, may hold values from -0.15625 to 0.15625
- footprint: int32 [512, 3], P(('groups', 'tile')), parts along dimension 0, may hold values from 0 to 4, all different within a row
- live: int32 [16], P(('groups', 'tile')), parts along dimension 0, may hold values from 1 to 32, as said below
- noise_weight: float32 [512, 128], P(('groups', 'tile')), parts along dimension 0, may hold values from 0.25 to 4
- probes: bfloat16 [16, 512, 256], P(('groups', 'tile'), 'col'), parts along dimension 0, may hold values from -6 to 6
Outputs:
- basis: float32 [16, 512, 256], P(('groups', 'tile'), 'col'), parts along dimension 0
- factor: float32 [512, 256], P('groups'), parts along dimension 0
There are 2 independent parts, one for each index of `groups`. A program takes and returns all parts, laid end to end along the dimension named above; each array names one. Nothing has to cross between parts.
Inputs may be any that keep to these rules, and one draw needn't show every extreme that they name: `footprint`: each row lists 3 different offsets. Some band has all 32 slots live.
All inputs are finite; a program needn't handle non-finite values.
Results may differ from a plain program's by a relative error of at most 0.0014.
Values may be sent and summed in bfloat16 or wider, within the bound.
A program may use at most 64 MiB of HBM per device.

v0:
```python
import math

import jax
import jax.numpy as jnp
from jax import lax
from jax.sharding import PartitionSpec as P


def shifted(value, axis, steps):
    count = lax.axis_size(axis)
    pairs = [(source, (source + steps) % count) for source in range(count)]
    return lax.ppermute(value, axis, pairs)


def neighbour(piece, offset):
    return shifted(piece, "tile", offset)


def on_device(jacobian, footprint, live, noise_weight, probes):
    slots, reach, rows, cells = jacobian.shape
    width = probes.shape[2]
    group = math.gcd(slots, 8)
    turns = slots // group
    window = jnp.concatenate(
        [
            neighbour(probes, 2),
            neighbour(probes, 1),
            probes,
            neighbour(probes, -1),
            neighbour(probes, -2),
        ],
        axis=0,
    )
    onehot = footprint[:, :, None] == jnp.arange(5, dtype=jnp.int32)[None, None, :]
    hot_narrow = onehot.astype(jnp.bfloat16).reshape(turns, group, reach, 5)
    hot_wide = onehot.astype(jnp.float32).reshape(turns, group, reach, 5)
    jac_groups = jacobian.reshape(turns, group, reach, rows, cells)

    def forward(carry, inputs):
        jac_part, hot_part = inputs
        picked = jnp.einsum(
            "gfo,ock->gfck", hot_part, window, preferred_element_type=jnp.float32
        ).astype(jnp.bfloat16)
        images = jnp.einsum("gfrc,gfck->grk", jac_part, picked, preferred_element_type=jnp.float32)
        return (carry, images)

    _, partial_value = lax.scan(forward, jnp.zeros((), jnp.float32), (jac_groups, hot_narrow))
    partial_value = partial_value.reshape(slots, rows, width)
    active = (jnp.arange(slots, dtype=jnp.int32) < live[0]).astype(jnp.float32)
    scaling = noise_weight * active[:, None]
    share = lax.psum_scatter(partial_value, "col", scatter_dimension=1, tiled=True)
    half = share.shape[1]
    local_scale = lax.dynamic_slice_in_dim(scaling, lax.axis_index("col") * half, half, 1)
    piece = (share * local_scale[:, :, None]).astype(jnp.bfloat16)
    weighted = lax.all_gather(piece, "col", axis=1, tiled=True)
    weighted_groups = weighted.reshape(turns, group, rows, width)

    def backward(bucket, inputs):
        jac_part, hot_part, weighted_part = inputs
        contrib = jnp.einsum(
            "gfrc,grk->gfck", jac_part, weighted_part, preferred_element_type=jnp.float32
        )
        added = jnp.einsum("gfo,gfck->ock", hot_part, contrib, precision=lax.Precision.HIGHEST)
        return (bucket + added, None)

    bucket, _ = lax.scan(
        backward, jnp.zeros((5, cells, width), jnp.float32), (jac_groups, hot_wide, weighted_groups)
    )
    total = bucket[2]
    for offset in (-2, -1, 1, 2):
        total = total + shifted(bucket[2 + offset], "tile", offset)
    field = probes[0].astype(jnp.float32) + total
    local_gram = jnp.dot(field.T, field, precision=lax.Precision.HIGHEST)
    gram = lax.psum(local_gram, ("tile", "col"))
    lower = jnp.linalg.cholesky(gram)
    states = cells * lax.axis_size("col") * lax.axis_size("tile")
    scale = math.sqrt(states)
    solved = jax.scipy.linalg.solve_triangular(lower, field.T, lower=True)
    basis = (solved.T * scale)[None]
    factor = lower.T / scale
    return (basis, factor)


def solution(mesh):
    placed = (
        P(("groups", "tile"), None, None, "col"),
        P(("groups", "tile"), None),
        P(("groups", "tile")),
        P(("groups", "tile"), None),
        P(("groups", "tile"), "col", None),
    )
    return jax.shard_map(
        on_device,
        mesh=mesh,
        in_specs=placed,
        out_specs=(P(("groups", "tile"), "col", None), P("groups", None)),
        check_vma=False,
    )
```

profile of v0, /device:TPU:0, one launch (start us, length us, event | category | flops | bytes accessed | tf_op | source)
XLA Modules:
  0.0 315.2 jit_solution(8248134718715111169)
XLA Ops:
  7.2 3.1 collective-permute-start
  10.3 1.5 collective-permute-start.1
  11.8 3.2 %collective-permute-start.2 = (bf16[1,256,256]{2,1,0:T(8,128)(2,1)}, bf16[1,256,256]{2,1,0:T(8,128)(2,1)S(1)}, u32[]{:S(2)}, u32[]{:S(2)}) collective-permute-start(bf16[1,256,256]{2,1,0:T(8,128)(2,1)} %param.13), channel_id=1, source_target_pairs={{0,14},{2,0},{4,2},{6,4},{8,6},{10,8},{12,10},{14,12},{1,15},{3,1}... | collective-permute-start | bytes 393224 | tf_op jit(solution)/shard_map/ppermute | solution.py:12
  15.0 0.3 collective-permute-start.3
  15.3 0.8 eq.17
  16.1 0.3 collective-permute-done
  16.4 4.4 %collective-permute-done.1 = bf16[1,256,256]{2,1,0:T(8,128)(2,1)S(1)} collective-permute-done((bf16[1,256,256]{2,1,0:T(8,128)(2,1)}, bf16[1,256,256]{2,1,0:T(8,128)(2,1)S(1)}, u32[]{:S(2)}, u32[]{:S(2)}) %collective-permute-start.1) | collective-permute-done | bytes 131104 | tf_op jit(solution)/shard_map/ppermute | solution.py:12
  20.9 0.9 constant_dynamic-update-slice_fusion.2
  21.9 17.7 %while.22 = (s32[]{:T(128)}, f32[4,8,128,256]{3,2,1,0:T(8,128)}, bf16[4,8,3,128,256]{4,3,2,1,0:T(8,128)(2,1)}, bf16[4,8,3,5]{1,2,3,0:T(4,128)(2,1)S(1)}, bf16[5,256,256]{2,1,0:T(8,128)(2,1)S(1)}, /*index=5*/s32[]{:T(128)}) while((s32[]{:T(128)}, f32[4,8,128,256]{3,2,1,0:T(8,128)}, bf16[4,8,3,128,256]{4,3,2,1,0:T(8,128)(2,1)}, ...), condition=%wide.region_1.2_spmd, body=%wide.region_0.1_spmd.sunk | while | flops 418381824 | bytes 9570073 | solution.py:47
  21.9 1.3 fusion.64
  23.2 3.1 fusion.65
  26.3 1.3 fusion.64
  27.6 3.1 fusion.65
  30.7 1.3 fusion.64
  32.0 3.1 fusion.65
  35.1 1.3 fusion.64
  36.4 3.1 fusion.65
  39.6 0.0 all-gather.2.cloned.1.call-start
  40.3 0.1 dynamic-slice_multiply_fusion
  40.4 11.5 %reduce-scatter.2.cloned.1.call-done = f32[32,64,256]{2,1,0:T(8,128)} async-done(((f32[32,128,256]{2,1,0:T(8,128)}), f32[32,64,256]{2,1,0:T(8,128)}) %reduce-scatter.2.cloned.1.call-update) | async-done | bytes 2097168 | tf_op jit(solution)/shard_map/reduce_scatter | solution.py:51
  51.8 2.9 multiply_convert_fusion
  54.8 0.0 all-reduce.3.cloned.1.call-start
  54.8 11.9 %all-gather.2.cloned.1.call-done = bf16[32,128,256]{2,1,0:T(8,128)(2,1)} async-done(((bf16[32,64,256]{2,1,0:T(8,128)(2,1)}), bf16[32,128,256]{2,1,0:T(8,128)(2,1)}) %all-gather.2.cloned.1.call-update) | async-done | bytes 2097168 | tf_op jit(solution)/shard_map/all_gather | solution.py:55
  66.8 62.4 %while.24 = (s32[]{:T(128)}, f32[5,256,256]{2,0,1:T(8,128)S(1)}, f32[4,8,3,5]{1,2,3,0:T(4,128)S(1)}, bf16[4,8,3,128,256]{4,3,2,1,0:T(8,128)(2,1)}, bf16[4,8,128,256]{3,2,1,0:T(8,128)(2,1)}, /*index=5*/s32[]{:T(128)}, s32[]{:T(128)}) while((s32[]{:T(128)}, f32[5,256,256]{2,0,1:T(8,128)S(1)}, f32[4,8,3,5]{1,2,3,0:T(4,128)S(1)}, ...), condition=%wide.region_4.5_spmd.clone, body=%wide.region_3.4_spmd.clone.sunk | while | flops 497680384 | bytes 17304060 | solution.py:66
  66.8 5.2 %fusion.71 = f32[8,3,256,256]{3,2,1,0:T(8,128)} fusion(bf16[4,8,3,128,256]{4,3,2,1,0:T(8,128)(2,1)} %get-tuple-element.257, s32[]{:T(128)} %get-tuple-element.247, bf16[4,8,128,256]{3,2,1,0:T(8,128)(2,1)} %get-tuple-element.258), kind=kOutput, calls=%fused_computation.16.clone.1 | convolution fusion | flops 402653184 | bytes 8389632 | tf_op jit(solution)/shard_map/while/body/eval_jaxpr/gfrc,grk->gfck/dot_general | solution.py:60
  72.0 10.4 %bitcast_add_fusion.3 = f32[5,256,256]{2,0,1:T(8,128)S(1)} fusion(f32[5,256,256]{2,0,1:T(8,128)S(1)} %get-tuple-element.248, f32[8,3,256,256]{3,2,1,0:T(8,128)} %fusion.71, pred[]{:T(512)S(6)} %compare.27, f32[8,3,5]{0,1,2:T(4,128)S(1)} %dynamic-slice_bitcast_fusion.5), kind=kOutput, calls=%fused_computation.15.clone.1 | convolution fusion | flops 95027200 | bytes 8913377 | tf_op jit(solution)/shard_map/while/body/eval_jaxpr/gfo,gfck->ock/dot_general | solution.py:63
  82.4 5.2 %fusion.71 = f32[8,3,256,256]{3,2,1,0:T(8,128)} fusion(bf16[4,8,3,128,256]{4,3,2,1,0:T(8,128)(2,1)} %get-tuple-element.257, s32[]{:T(128)} %get-tuple-element.247, bf16[4,8,128,256]{3,2,1,0:T(8,128)(2,1)} %get-tuple-element.258), kind=kOutput, calls=%fused_computation.16.clone.1 | convolution fusion | flops 402653184 | bytes 8389632 | tf_op jit(solution)/shard_map/while/body/eval_jaxpr/gfrc,grk->gfck/dot_general | solution.py:60
  87.6 10.4 %bitcast_add_fusion.3 = f32[5,256,256]{2,0,1:T(8,128)S(1)} fusion(f32[5,256,256]{2,0,1:T(8,128)S(1)} %get-tuple-element.248, f32[8,3,256,256]{3,2,1,0:T(8,128)} %fusion.71, pred[]{:T(512)S(6)} %compare.27, f32[8,3,5]{0,1,2:T(4,128)S(1)} %dynamic-slice_bitcast_fusion.5), kind=kOutput, calls=%fused_computation.15.clone.1 | convolution fusion | flops 95027200 | bytes 8913377 | tf_op jit(solution)/shard_map/while/body/eval_jaxpr/gfo,gfck->ock/dot_general | solution.py:63
  97.9 5.2 %fusion.71 = f32[8,3,256,256]{3,2,1,0:T(8,128)} fusion(bf16[4,8,3,128,256]{4,3,2,1,0:T(8,128)(2,1)} %get-tuple-element.257, s32[]{:T(128)} %get-tuple-element.247, bf16[4,8,128,256]{3,2,1,0:T(8,128)(2,1)} %get-tuple-element.258), kind=kOutput, calls=%fused_computation.16.clone.1 | convolution fusion | flops 402653184 | bytes 8389632 | tf_op jit(solution)/shard_map/while/body/eval_jaxpr/gfrc,grk->gfck/dot_general | solution.py:60
  103.2 10.4 %bitcast_add_fusion.3 = f32[5,256,256]{2,0,1:T(8,128)S(1)} fusion(f32[5,256,256]{2,0,1:T(8,128)S(1)} %get-tuple-element.248, f32[8,3,256,256]{3,2,1,0:T(8,128)} %fusion.71, pred[]{:T(512)S(6)} %compare.27, f32[8,3,5]{0,1,2:T(4,128)S(1)} %dynamic-slice_bitcast_fusion.5), kind=kOutput, calls=%fused_computation.15.clone.1 | convolution fusion | flops 95027200 | bytes 8913377 | tf_op jit(solution)/shard_map/while/body/eval_jaxpr/gfo,gfck->ock/dot_general | solution.py:63
  113.5 5.2 %fusion.71 = f32[8,3,256,256]{3,2,1,0:T(8,128)} fusion(bf16[4,8,3,128,256]{4,3,2,1,0:T(8,128)(2,1)} %get-tuple-element.257, s32[]{:T(128)} %get-tuple-element.247, bf16[4,8,128,256]{3,2,1,0:T(8,128)(2,1)} %get-tuple-element.258), kind=kOutput, calls=%fused_computation.16.clone.1 | convolution fusion | flops 402653184 | bytes 8389632 | tf_op jit(solution)/shard_map/while/body/eval_jaxpr/gfrc,grk->gfck/dot_general | solution.py:60
  118.7 10.4 %bitcast_add_fusion.3 = f32[5,256,256]{2,0,1:T(8,128)S(1)} fusion(f32[5,256,256]{2,0,1:T(8,128)S(1)} %get-tuple-element.248, f32[8,3,256,256]{3,2,1,0:T(8,128)} %fusion.71, pred[]{:T(512)S(6)} %compare.27, f32[8,3,5]{0,1,2:T(4,128)S(1)} %dynamic-slice_bitcast_fusion.5), kind=kOutput, calls=%fused_computation.15.clone.1 | convolution fusion | flops 95027200 | bytes 8913377 | tf_op jit(solution)/shard_map/while/body/eval_jaxpr/gfo,gfck->ock/dot_general | solution.py:63
  129.1 0.4 copy.9
  129.6 0.3 slice.64
  129.9 0.1 slice_bitcast_fusion.2
  129.9 3.6 %collective-permute-start.4 = (f32[256,256]{1,0:T(8,128)S(1)}, f32[256,256]{1,0:T(8,128)S(1)}, u32[]{:S(2)}, u32[]{:S(2)}) collective-permute-start(f32[256,256]{1,0:T(8,128)S(1)} %get-tuple-element.116), channel_id=1, source_target_pairs={{0,12},{2,14},{4,0},{6,2},{8,4},{10,6},{12,8},{14,10},{1,13},{3,15... | collective-permute-start | bytes 786440 | tf_op jit(solution)/shard_map/ppermute | solution.py:12
  133.6 1.5 collective-permute-start.6
  135.1 3.5 %collective-permute-start.5 = (f32[256,256]{1,0:T(8,128)S(1)}, f32[256,256]{1,0:T(8,128)S(1)}, u32[]{:S(2)}, u32[]{:S(2)}) collective-permute-start(f32[256,256]{1,0:T(8,128)S(1)} %bitcast.127), channel_id=1, source_target_pairs={{0,14},{2,0},{4,2},{6,4},{8,6},{10,8},{12,10},{14,12},{1,15},{3,1}... | collective-permute-start | bytes 786440 | tf_op jit(solution)/shard_map/ppermute | solution.py:12
  138.5 1.8 collective-permute-done.4
  140.3 7.5 %collective-permute-done.6 = f32[256,256]{1,0:T(8,128)S(1)} collective-permute-done((f32[256,256]{1,0:T(8,128)S(1)}, f32[256,256]{1,0:T(8,128)S(1)}, u32[]{:S(2)}, u32[]{:S(2)}) %collective-permute-start.6) | collective-permute-done | bytes 262176 | tf_op jit(solution)/shard_map/ppermute | solution.py:12
  147.8 3.0 collective-permute-done.5
  150.9 0.1 fusion.29
  151.0 1.3 fusion.44
  152.3 91.8 %all-reduce.3.cloned.1.call-done = f32[256,256]{0,1:T(8,128)} async-done(((f32[256,256]{0,1:T(8,128)}), f32[256,256]{0,1:T(8,128)}) %all-reduce.3.cloned.1.call-update) | async-done | bytes 262160 | tf_op jit(solution)/shard_map/psum | solution.py:74
  244.1 1.1 copy.14
  245.2 1.0 fusion.31
  246.2 11.7 %cholesky.50 = f32[128,128]{1,0:T(8,128)S(1)} custom-call(f32[128,128]{1,0:T(8,128)S(1)} %cholesky.118), custom_call_target="Cholesky" | custom-call | tf_op jit(solution)/shard_map/jit(cholesky)/cholesky | solution.py:75
  258.0 9.8 %custom-call.15 = f32[1,128,128]{1,2,0:T(8,128)S(1)} custom-call(f32[1,128,128]{2,1,0:T(8,128)S(1)} %get-tuple-element.124), custom_call_target="InvertDiagBlocksLowerTriangular" | custom-call | tf_op jit(solution)/shard_map/jit(cholesky)/cholesky | solution.py:75
  267.8 0.2 constant_dynamic-update-slice_fusion.6
  268.0 0.3 convolution_subtract_fusion
  268.3 11.7 %cholesky.105 = f32[128,128]{1,0:T(8,128)S(1)} custom-call(f32[128,128]{1,0:T(8,128)S(1)} %convolution_subtract_fusion), custom_call_target="Cholesky" | custom-call | tf_op jit(solution)/shard_map/jit(cholesky)/cholesky | solution.py:75
  280.0 0.7 compare_reduce_fusion
  282.0 0.1 triangular_solve.57
  282.1 4.1 %while.23 = (s32[]{:T(128)}, f32[256,256]{1,0:T(8,128)S(1)}, s32[2,2]{1,0:T(2,128)S(1)}, f32[2,128,128]{2,1,0:T(8,128)S(1)}, s32[]{:T(128)}) while((s32[]{:T(128)}, f32[256,256]{1,0:T(8,128)S(1)}, s32[2,2]{1,0:T(2,128)S(1)}, f32[2,128,128]{2,1,0:T(8,128)S(1)}, s32[]{:T(128)}) %tuple.68), condition=%wide.while_cond, body=%wide.while_body.sunk | while | flops 2 | bytes 131181 | solution.py:78
  282.3 0.6 fusion.66
  282.9 1.4 bitcast_dynamic-update-slice_fusion.2
  284.3 0.6 fusion.66
  284.8 1.4 bitcast_dynamic-update-slice_fusion.2
  286.2 19.7 %custom-call.16 = f32[2,128,128]{1,2,0:T(8,128)S(1)} custom-call(f32[2,128,128]{2,1,0:T(8,128)S(1)} %get-tuple-element.65), custom_call_target="InvertDiagBlocksLowerTriangular" | custom-call | tf_op jit(solution)/shard_map/jit(_solve_triangular)/triangular_solve | solution.py:78
  305.9 0.3 fusion.34
  306.2 0.4 fusion.36
  306.6 0.3 fusion.33
  307.0 0.8 copy.15
  307.8 0.8 copy.16
  (40 shorter events, 0.4 us)
Async XLA Ops:
  7.2 44.7 %reduce-scatter.2.cloned.1.call-start = ((), (), s32[]{:S(2)}) async-start(), calls=%async_computation.1 | async-start | bytes 6291456 | tf_op jit(solution)/shard_map/reduce_scatter | solution.py:51
  7.2 9.2 %collective-permute-start = (bf16[1,256,256]{2,1,0:T(8,128)(2,1)}, bf16[1,256,256]{2,1,0:T(8,128)(2,1)S(1)}, u32[]{:S(2)}, u32[]{:S(2)}) collective-permute-start(bf16[1,256,256]{2,1,0:T(8,128)(2,1)} %param.13), channel_id=1, source_target_pairs={{0,4},{2,6},{4,8},{6,10},{8,12},{10,14},{12,0},{14,2},{1,5},{3,7},... | collective-permute-start | bytes 393224 | tf_op jit(solution)/shard_map/ppermute | solution.py:12
  10.3 10.6 %collective-permute-start.1 = (bf16[1,256,256]{2,1,0:T(8,128)(2,1)}, bf16[1,256,256]{2,1,0:T(8,128)(2,1)S(1)}, u32[]{:S(2)}, u32[]{:S(2)}) collective-permute-start(bf16[1,256,256]{2,1,0:T(8,128)(2,1)} %param.13), channel_id=1, source_target_pairs={{0,2},{2,4},{4,6},{6,8},{8,10},{10,12},{12,14},{14,0},{1,3},{3,5},... | collective-permute-start | bytes 393224 | tf_op jit(solution)/shard_map/ppermute | solution.py:12
  11.8 10.0 %collective-permute-start.2 = (bf16[1,256,256]{2,1,0:T(8,128)(2,1)}, bf16[1,256,256]{2,1,0:T(8,128)(2,1)S(1)}, u32[]{:S(2)}, u32[]{:S(2)}) collective-permute-start(bf16[1,256,256]{2,1,0:T(8,128)(2,1)} %param.13), channel_id=1, source_target_pairs={{0,14},{2,0},{4,2},{6,4},{8,6},{10,8},{12,10},{14,12},{1,15},{3,1}... | collective-permute-start | bytes 393224 | tf_op jit(solution)/shard_map/ppermute | solution.py:12
  15.0 6.8 %collective-permute-start.3 = (bf16[1,256,256]{2,1,0:T(8,128)(2,1)}, bf16[1,256,256]{2,1,0:T(8,128)(2,1)S(1)}, u32[]{:S(2)}, u32[]{:S(2)}) collective-permute-start(bf16[1,256,256]{2,1,0:T(8,128)(2,1)} %param.13), channel_id=1, source_target_pairs={{0,12},{2,14},{4,0},{6,2},{8,4},{10,6},{12,8},{14,10},{1,13},{3,15... | collective-permute-start | bytes 393224 | tf_op jit(solution)/shard_map/ppermute | solution.py:12
  39.5 0.7 copy-start.1
  39.6 27.2 %all-gather.2.cloned.1.call-start = ((), (), s32[]{:S(2)}) async-start(), calls=%async_computation.2 | async-start | bytes 3145728 | tf_op jit(solution)/shard_map/all_gather | solution.py:55
  54.8 189.3 %all-reduce.3.cloned.1.call-start = ((), (), s32[]{:S(2)}) async-start(), calls=%async_computation.3 | async-start | bytes 524288 | tf_op jit(solution)/shard_map/psum | solution.py:74
  129.1 21.7 %copy-start = (bf16[1,256,256]{2,1,0:T(8,128)(2,1)S(1)}, bf16[1,256,256]{2,1,0:T(8,128)(2,1)}, u32[]{:S(2)}) copy-start(bf16[1,256,256]{2,1,0:T(8,128)(2,1)} %param.13) | copy-start | bytes 393220
  129.9 10.4 %collective-permute-start.4 = (f32[256,256]{1,0:T(8,128)S(1)}, f32[256,256]{1,0:T(8,128)S(1)}, u32[]{:S(2)}, u32[]{:S(2)}) collective-permute-start(f32[256,256]{1,0:T(8,128)S(1)} %get-tuple-element.116), channel_id=1, source_target_pairs={{0,12},{2,14},{4,0},{6,2},{8,4},{10,6},{12,8},{14,10},{1,13},{3,15... | collective-permute-start | bytes 786440 | tf_op jit(solution)/shard_map/ppermute | solution.py:12
  133.6 14.2 %collective-permute-start.6 = (f32[256,256]{1,0:T(8,128)S(1)}, f32[256,256]{1,0:T(8,128)S(1)}, u32[]{:S(2)}, u32[]{:S(2)}) collective-permute-start(f32[256,256]{1,0:T(8,128)S(1)} %get-tuple-element.118), channel_id=1, source_target_pairs={{0,2},{2,4},{4,6},{6,8},{8,10},{10,12},{12,14},{14,0},{1,3},{3,5},... | collective-permute-start | bytes 786440 | tf_op jit(solution)/shard_map/ppermute | solution.py:12
  135.0 12.8 %collective-permute-start.7 = (f32[256,256]{1,0:T(8,128)S(1)}, f32[256,256]{1,0:T(8,128)S(1)}, u32[]{:S(2)}, u32[]{:S(2)}) collective-permute-start(f32[256,256]{1,0:T(8,128)S(1)} %get-tuple-element.117), channel_id=1, source_target_pairs={{0,4},{2,6},{4,8},{6,10},{8,12},{10,14},{12,0},{14,2},{1,5},{3,7},... | collective-permute-start | bytes 786440 | tf_op jit(solution)/shard_map/ppermute | solution.py:12
  135.1 15.8 %collective-permute-start.5 = (f32[256,256]{1,0:T(8,128)S(1)}, f32[256,256]{1,0:T(8,128)S(1)}, u32[]{:S(2)}, u32[]{:S(2)}) collective-permute-start(f32[256,256]{1,0:T(8,128)S(1)} %bitcast.127), channel_id=1, source_target_pairs={{0,14},{2,0},{4,2},{6,4},{8,6},{10,8},{12,10},{14,12},{1,15},{3,1}... | collective-permute-start | bytes 786440 | tf_op jit(solution)/shard_map/ppermute | solution.py:12
Sparse Core Ops, SparseCore 0:
  39.7 12.0 reduce-scatter.1
  54.9 11.8 all-gather.1
  152.4 91.6 all-reduce.2
where the time goes:
time: 316 us; the launch traced here: 315 us
  waiting for transfers between devices  132 us (42%)
  matrix products  82.6 us (26%)
  other arithmetic  57.8 us (18%)
  starting transfers between devices  16.9 us (5%)
  between operations  15.9 us (5%)
  local copies, waits for them, and re-layouts  9.31 us (3%)
    psum x1, waiting for transfers between devices, on_device(): gram = lax.psum(local_gram, ('tile', 'col'))  91.8 us
    dot_general x4, matrix products, backward(): jnp.einsum('gfo,gfck->ock', hot_part, contrib, precision=lax.Precision.HI...  41.5 us
    another operation x6, other arithmetic, on_device(): lower = jnp.linalg.cholesky(gram)  34 us
    dot_general x4, matrix products, backward(): jnp.einsum('gfrc,grk->gfck', jac_part, weighted_part, preferred_element_t...  20.8 us
    another operation x2, other arithmetic, on_device(): solved = jax.scipy.linalg.solve_triangular(lower, field.T, lower=True)  19.7 us
    ppermute x8, waiting for transfers between devices, shifted(): return lax.ppermute(value, axis, pairs)  17.1 us
    ppermute x8, starting transfers between devices, shifted(): return lax.ppermute(value, axis, pairs)  16.7 us
    dot_general x4, matrix products, forward(): jnp.einsum('gfrc,gfck->grk', jac_part, picked, preferred_element_type=jnp...  12.5 us
  transfers between devices with their start and end apart: 11, of which 8 were waited for; matrix products, arithmetic and copies ran while one was open for 1% of the time, Pallas kernels for 0%

commit v1 on v0

v1 whole, which is shorter than its diff:
```python
import functools
import math

import jax
import jax.numpy as jnp
from jax import lax
from jax.experimental import pallas as pl
from jax.experimental.pallas import tpu as pltpu
from jax.sharding import PartitionSpec as P

MESH = pl.DeviceIdType.MESH
REACH = 5
VMEM = pl.BlockSpec(memory_space=pltpu.VMEM)
ANY = pl.BlockSpec(memory_space=pl.ANY)
HIGHEST = lax.Precision.HIGHEST


def remote(src, dst, send, recv, where):
    return pltpu.make_async_remote_copy(
        src_ref=src, dst_ref=dst, send_sem=send, recv_sem=recv,
        device_id=where, device_id_type=MESH,
    )


def greet(devices):
    barrier = pltpu.get_barrier_semaphore()
    for where in devices:
        pl.semaphore_signal(barrier, inc=1, device_id=where, device_id_type=MESH)
    pl.semaphore_wait(barrier, len(devices))


def ring(bands):
    me = lax.axis_index("tile")
    odd = lax.rem(me, 2)
    mate = me + 1 - 2 * odd
    up = lax.rem(me + 2, bands)
    down = lax.rem(me + bands - 2, bands)
    return me, odd, mate, up, down


def window_kernel(bands, probes, window, send, recv):
    me, odd, mate, up, down = ring(bands)
    greet([{"tile": mate}, {"tile": up}, {"tile": down}])
    own = probes.at[0]
    hops = [
        remote(own, window.at[0], send.at[0], recv.at[0], {"tile": up}),
        remote(own, window.at[4], send.at[1], recv.at[1], {"tile": down}),
        remote(own, window.at[1 + 2 * odd], send.at[2], recv.at[2], {"tile": mate}),
        remote(window.at[4 - 4 * odd], window.at[3 - 2 * odd], send.at[3], recv.at[3], {"tile": mate}),
    ]
    for hop in hops[:3]:
        hop.start()
    window[2] = probes[0]
    hops[0].wait_recv()
    hops[1].wait_recv()
    hops[3].start()
    hops[2].wait_recv()
    hops[3].wait_recv()
    for hop in hops:
        hop.wait_send()


def fetch_window(probes, bands):
    _, cells, width = probes.shape
    return pl.pallas_call(
        functools.partial(window_kernel, bands),
        out_shape=jax.ShapeDtypeStruct((REACH, cells, width), probes.dtype),
        in_specs=[VMEM],
        out_specs=VMEM,
        scratch_shapes=[pltpu.SemaphoreType.DMA((4,)), pltpu.SemaphoreType.DMA((4,))],
        compiler_params=pltpu.CompilerParams(collective_id=0, has_side_effects=True),
        name="fetch_window",
    )(probes)


def forward_kernel(group, reach, foot, jac, window, out, turned):
    step = pl.program_id(0)

    @pl.when(step == 0)
    def _():
        for o in range(REACH):
            turned[o] = window[o].astype(jnp.float32).T.astype(turned.dtype)

    for g in range(group):
        total = None
        for f in range(reach):
            o = foot[(step * group + g) * reach + f]
            part = lax.dot_general(
                turned[o], jac[g, f], (((1,), (1,)), ((), ())), preferred_element_type=jnp.float32
            )
            total = part if total is None else total + part
        out[g] = total


def forward(foot, jacobian, window, group):
    slots, reach, rows, cells = jacobian.shape
    width = window.shape[2]
    return pl.pallas_call(
        functools.partial(forward_kernel, group, reach),
        out_shape=jax.ShapeDtypeStruct((slots, width, rows), jnp.float32),
        grid_spec=pltpu.PrefetchScalarGridSpec(
            num_scalar_prefetch=1,
            grid=(slots // group,),
            in_specs=[
                pl.BlockSpec((group, reach, rows, cells), lambda i, foot: (i, 0, 0, 0)),
                pl.BlockSpec((REACH, cells, width), lambda i, foot: (0, 0, 0)),
            ],
            out_specs=pl.BlockSpec((group, width, rows), lambda i, foot: (i, 0, 0)),
            scratch_shapes=[pltpu.VMEM((REACH, width, cells), window.dtype)],
        ),
        name="forward_images",
    )(foot, jacobian, window)


def swap_kernel(value, other, send, recv):
    partner = {"col": 1 - lax.axis_index("col")}
    greet([partner])
    hop = remote(value, other, send, recv, partner)
    hop.start()
    hop.wait()


def swap_cores(value):
    return pl.pallas_call(
        swap_kernel,
        out_shape=jax.ShapeDtypeStruct(value.shape, value.dtype),
        in_specs=[ANY],
        out_specs=ANY,
        scratch_shapes=[pltpu.SemaphoreType.DMA, pltpu.SemaphoreType.DMA],
        compiler_params=pltpu.CompilerParams(collective_id=1, has_side_effects=True),
        name="swap_images",
    )(value)


def backward_kernel(group, reach, foot, live, jac, noise, mine, other, bucket):
    step = pl.program_id(0)

    @pl.when(step == 0)
    def _():
        bucket[...] = jnp.zeros_like(bucket)

    for g in range(group):
        slot = step * group + g
        active = jnp.where(slot < live[0], 1.0, 0.0).astype(jnp.float32)
        scale = noise[pl.ds(slot, 1), :] * active
        weighted = ((mine[g] + other[g]) * scale).astype(jnp.bfloat16)
        for f in range(reach):
            o = foot[slot * reach + f]
            bucket[o] += jnp.dot(weighted, jac[g, f], preferred_element_type=jnp.float32)


def backward(foot, live, jacobian, noise, mine, other, group):
    slots, reach, rows, cells = jacobian.shape
    width = mine.shape[1]
    return pl.pallas_call(
        functools.partial(backward_kernel, group, reach),
        out_shape=jax.ShapeDtypeStruct((REACH, width, cells), jnp.float32),
        grid_spec=pltpu.PrefetchScalarGridSpec(
            num_scalar_prefetch=2,
            grid=(slots // group,),
            in_specs=[
                pl.BlockSpec((group, reach, rows, cells), lambda i, foot, live: (i, 0, 0, 0)),
                pl.BlockSpec((slots, rows), lambda i, foot, live: (0, 0)),
                pl.BlockSpec((group, width, rows), lambda i, foot, live: (i, 0, 0)),
                pl.BlockSpec((group, width, rows), lambda i, foot, live: (i, 0, 0)),
            ],
            out_specs=pl.BlockSpec((REACH, width, cells), lambda i, foot, live: (0, 0, 0)),
        ),
        name="back_project",
    )(foot, live, jacobian, noise, mine, other)


def collect_kernel(bands, split, bucket, probes, field, gram, got, relay, half, mine, parts, full, whole,
                   send, recv, gsend, grecv, asend, arecv):
    me, odd, mate, up, down = ring(bands)
    core = lax.axis_index("col")
    partner = {"col": 1 - core}
    peers = [{"tile": lax.rem(me + d, bands)} for d in range(1, bands)]
    greet(peers + [partner])
    straight = {"tile": lax.rem(me + bands - 2 + 4 * odd, bands)}
    turned = {"tile": lax.rem(me + 2 + (bands - 4) * odd, bands)}
    hops = [
        remote(bucket.at[1 + 2 * odd], got.at[0], send.at[0], recv.at[0], {"tile": mate}),
        remote(bucket.at[4 * odd], got.at[2], send.at[1], recv.at[1], straight),
        remote(bucket.at[3 - 2 * odd], got.at[1], send.at[2], recv.at[2], {"tile": mate}),
        remote(relay, got.at[3], send.at[3], recv.at[3], turned),
    ]
    for hop in hops[:3]:
        hop.start()
    base = probes[0].astype(jnp.float32).T + bucket[2]
    hops[0].wait_recv()
    relay[...] = bucket[4 - 4 * odd] + got[0]
    hops[3].start()
    hops[2].wait_recv()
    base = base + got[1]
    hops[1].wait_recv()
    base = base + got[2]
    hops[3].wait_recv()
    field[...] = base + got[3]
    for hop in hops:
        hop.wait_send()
    value = field[...]
    local = lax.dot_general(
        value, value, (((1,), (1,)), ((), ())), precision=HIGHEST, preferred_element_type=jnp.float32
    )
    if not split:
        gram[...] = local
        return
    rows = half.shape[1]
    piece = rows // bands
    whole[0] = local[:rows]
    whole[1] = local[rows:]
    hop = remote(whole.at[1 - core], half.at[0], gsend.at[0], grecv.at[0], partner)
    hop.start()
    hop.wait()
    mine[...] = (whole[core] + half[0]).reshape(bands, piece, mine.shape[2])
    hops = []
    for d in range(1, bands):
        target = lax.rem(me + d, bands)
        hops.append(remote(mine.at[target], parts.at[d - 1], gsend.at[d], grecv.at[d], {"tile": target}))
    for hop in hops:
        hop.start()
    total = mine[me]
    for d in range(1, bands):
        hops[d - 1].wait_recv()
        total = total + parts[d - 1]
    for hop in hops:
        hop.wait_send()
    full[me] = total
    hops = []
    for d in range(1, bands):
        target = lax.rem(me + d, bands)
        hops.append(remote(full.at[me], full.at[me], asend.at[d], arecv.at[d], {"tile": target}))
    for hop in hops:
        hop.start()
    for hop in hops:
        hop.wait_recv()
    for hop in hops:
        hop.wait_send()
    hop = remote(full, gram.at[core], asend.at[0], arecv.at[0], partner)
    hop.start()
    gram[core] = full[...]
    hop.wait()


def collect(bucket, probes, bands, split):
    _, width, cells = bucket.shape
    rows = width // 2
    piece = rows // bands if split else 8
    gram_shape = (2, bands, piece, width) if split else (width, width)
    field, gram = pl.pallas_call(
        functools.partial(collect_kernel, bands, split),
        out_shape=(
            jax.ShapeDtypeStruct((width, cells), jnp.float32),
            jax.ShapeDtypeStruct(gram_shape, jnp.float32),
        ),
        in_specs=[VMEM, VMEM],
        out_specs=(VMEM, VMEM),
        scratch_shapes=[
            pltpu.VMEM((4, width, cells), jnp.float32),
            pltpu.VMEM((width, cells), jnp.float32),
            pltpu.VMEM((1, rows, width), jnp.float32),
            pltpu.VMEM((bands, piece, width), jnp.float32),
            pltpu.VMEM((bands - 1, piece, width), jnp.float32),
            pltpu.VMEM((bands, piece, width), jnp.float32),
            pltpu.VMEM((2, rows, width), jnp.float32),
            pltpu.SemaphoreType.DMA((4,)),
            pltpu.SemaphoreType.DMA((4,)),
            pltpu.SemaphoreType.DMA((bands,)),
            pltpu.SemaphoreType.DMA((bands,)),
            pltpu.SemaphoreType.DMA((bands,)),
            pltpu.SemaphoreType.DMA((bands,)),
        ],
        compiler_params=pltpu.CompilerParams(collective_id=2, has_side_effects=True),
        name="collect_gram",
    )(bucket, probes)
    return field, gram.reshape(width, width)


def eliminate(block):
    size = block.shape[0]
    groups = [block[8 * g : 8 * g + 8] for g in range(size // 8)]
    sub = lax.broadcasted_iota(jnp.int32, (8, 1), 0)
    for g in range(len(groups)):
        panel = groups[g]
        scaled = []
        for i in range(8):
            j = 8 * g + i
            r = lax.rsqrt(panel[i : i + 1, j : j + 1])
            upper = panel[i : i + 1, :] * r
            factor = jnp.where(sub > i, panel[:, j : j + 1] * r, 0.0)
            panel = jnp.where(sub == i, upper, panel - factor * upper)
            scaled.append((j, r, upper))
        groups[g] = panel
        for h in range(g + 1, len(groups)):
            rest = groups[h]
            for j, r, upper in scaled:
                rest = rest - (rest[:, j : j + 1] * r) * upper
            groups[h] = rest
    return jnp.concatenate(groups, axis=0)


def finish_kernel(scale, gram, field, basis, factor, inverse):
    width = gram.shape[0]
    half = width // 2
    row = lax.broadcasted_iota(jnp.int32, (half, half), 0)
    lane = lax.broadcasted_iota(jnp.int32, (half, half), 1)
    unit = jnp.where(row == lane, 1.0, 0.0).astype(jnp.float32)
    keep = lane >= row
    zeros = jnp.zeros((half, half), jnp.float32)
    top = eliminate(jnp.concatenate([gram[:half, :], unit], axis=1))
    side = top[:, half:width]
    inverse[:half, :half] = top[:, width:]
    inverse[:half, half:] = zeros
    factor[:half, :half] = jnp.where(keep, top[:, :half], 0.0) * (1.0 / scale)
    factor[:half, half:] = side * (1.0 / scale)
    change = jnp.dot(side.T, top[:, half:], precision=HIGHEST, preferred_element_type=jnp.float32)
    low = eliminate(
        jnp.concatenate([gram[half:, half:] - change[:, :half], -change[:, half:], unit], axis=1)
    )
    inverse[half:, :] = low[:, half:]
    factor[half:, half:] = jnp.where(keep, low[:, :half], 0.0) * (1.0 / scale)
    factor[half:, :half] = zeros
    solved = jnp.dot(inverse[...], field[...], precision=HIGHEST, preferred_element_type=jnp.float32)
    basis[0] = (solved * scale).T


def finish(gram, field, scale):
    width, cells = field.shape
    return pl.pallas_call(
        functools.partial(finish_kernel, scale),
        out_shape=(
            jax.ShapeDtypeStruct((1, cells, width), jnp.float32),
            jax.ShapeDtypeStruct((width, width), jnp.float32),
        ),
        in_specs=[VMEM, VMEM],
        out_specs=(VMEM, VMEM),
        scratch_shapes=[pltpu.VMEM((width, width), jnp.float32)],
        name="factor_solve",
    )(gram, field)


def on_device(jacobian, footprint, live, noise_weight, probes):
    slots = jacobian.shape[0]
    cells, width = probes.shape[1:]
    bands = lax.axis_size("tile")
    group = math.gcd(slots, 4)
    foot = footprint.reshape(-1)
    split = (width // 2) % (8 * bands) == 0
    window = fetch_window(probes, bands)
    mine = forward(foot, jacobian, window, group)
    other = swap_cores(mine)
    bucket = backward(foot, live, jacobian, noise_weight, mine, other, group)
    field, gram = collect(bucket, probes, bands, split)
    if not split:
        gram = lax.psum(gram, ("tile", "col"))
    scale = math.sqrt(cells * lax.axis_size("col") * bands)
    return finish(gram, field, scale)


def solution(mesh):
    placed = (
        P(("groups", "tile"), None, None, "col"),
        P(("groups", "tile"), None),
        P(("groups", "tile")),
        P(("groups", "tile"), None),
        P(("groups", "tile"), "col", None),
    )
    return jax.shard_map(
        on_device,
        mesh=mesh,
        in_specs=placed,
        out_specs=(P(("groups", "tile"), "col", None), P("groups", None)),
        check_vma=False,
    )
```

time: 316 us -> 107 us (0.34)
  waiting for transfers between devices: 132 us -> 0 us
  Pallas kernels: 0 us -> 103 us
  matrix products: 82.6 us -> 0 us
  other arithmetic: 57.8 us -> 0 us
  starting transfers between devices: 16.9 us -> 0 us
  between operations: 15.9 us -> 1.3 us
  local copies, waits for them, and re-layouts: 9.31 us -> 1.38 us
    pallas_call x0 -> x6, Pallas kernels: none -> 103 us  [the longest x1 33.8 us: collect(): pl.pallas_call(functools.partial(collect_kernel, bands, split), out_shape...]
    psum x1 -> x0, waiting for transfers between devices: 91.8 us -> none  [on_device(): gram = lax.psum(local_gram, ('tile', 'col'))]
    dot_general x17 -> x0, matrix products: 81.1 us -> none  [the longest x4 41.5 us: backward(): jnp.einsum('gfo,gfck->ock', hot_part, contrib, precision=lax.Precision.HI...]
    another operation x8 -> x0, other arithmetic: 53.7 us -> none  [the longest x6 34 us: on_device(): lower = jnp.linalg.cholesky(gram)]
    ppermute x8 -> x0, waiting for transfers between devices: 17.1 us -> none  [shifted(): return lax.ppermute(value, axis, pairs)]
    ppermute x8 -> x0, starting transfers between devices: 16.7 us -> none  [shifted(): return lax.ppermute(value, axis, pairs)]
    all_gather x1 -> x0, waiting for transfers between devices: 11.9 us -> none  [on_device(): weighted = lax.all_gather(piece, 'col', axis=1, tiled=True)]
    reduce_scatter x1 -> x0, waiting for transfers between devices: 11.5 us -> none  [on_device(): lax.psum_scatter(partial_value, 'col', scatter_dimension=1, tiled=True)]
  transfers between devices with their start and end apart: 11 -> 0, of which waited for: 8 -> 0; matrix products, arithmetic and copies ran while one was open for 1% -> 0% of each run, Pallas kernels for 0% -> 0%
where the time goes in v1:
time: 107 us; the launch traced here: 106 us
  Pallas kernels  103 us (96%)
  local copies, waits for them, and re-layouts  1.38 us (1%)
  between operations  1.3 us (1%)
    pallas_call x1, Pallas kernels, collect(): pl.pallas_call(functools.partial(collect_kernel, bands, split), out_shape...  33.8 us
    pallas_call x1, Pallas kernels, finish(): pl.pallas_call(functools.partial(finish_kernel, scale), out_shape=(jax.Sh...  24.1 us
    pallas_call x1, Pallas kernels, fetch_window(): pl.pallas_call(functools.partial(window_kernel, bands), out_shape=jax.Sha...  16.9 us
    pallas_call x1, Pallas kernels, backward(): pl.pallas_call(functools.partial(backward_kernel, group, reach), out_shap...  11.1 us
    pallas_call x1, Pallas kernels, forward(): pl.pallas_call(functools.partial(forward_kernel, group, reach), out_shape...  10.1 us
    pallas_call x1, Pallas kernels, swap_cores(): pl.pallas_call(swap_kernel, out_shape=jax.ShapeDtypeStruct(value.shape, v...  7.52 us

profile of v1, /device:TPU:0, one launch (start us, length us, event | category | flops | bytes accessed | tf_op | source)
XLA Modules:
  0.0 106.2 jit_solution(12471473030177541124)
XLA Ops:
  1.3 0.8 copy.8
  2.0 0.6 reshape.10.foot
  2.7 16.9 %fetch_window.1.window = bf16[5,256,256]{2,1,0:T(8,128)(2,1)} custom-call(bf16[1,256,256]{2,1,0:T(8,128)(2,1)} %probes.3), custom_call_target="tpu_custom_call" | custom-call | tf_op jit(solution)/shard_map/fetch_window/pallas_call | solution.py:65
  19.6 10.1 %forward_images.1.value.mine = f32[32,256,128]{2,1,0:T(8,128)} custom-call(s32[96]{0:T(128)} %reshape.10.foot, bf16[32,3,128,256]{3,2,1,0:T(8,128)(2,1)} %jac.3, bf16[5,256,256]{2,1,0:T(8,128)(2,1)} %fetch_window.1.window), custom_call_target="tpu_custom_call" | custom-call | tf_op jit(solution)/shard_map/forward_images/pallas_call | solution.py:98
  29.7 7.5 %swap_images.1.other = f32[32,256,128]{2,1,0:T(8,128)} custom-call(f32[32,256,128]{2,1,0:T(8,128)} %forward_images.1.value.mine), custom_call_target="tpu_custom_call" | custom-call | tf_op jit(solution)/shard_map/swap_images/pallas_call | solution.py:124
  37.2 11.1 %back_project.1.bucket = f32[5,256,256]{2,1,0:T(8,128)} custom-call(s32[96]{0:T(128)} %reshape.10.foot, s32[1]{0:T(128)S(6)} %copy.9.live, bf16[32,3,128,256]{3,2,1,0:T(8,128)(2,1)} %jac.3, f32[32,128]{1,0:T(8,128)} %noise.1, f32[32,256,128]{2,1,0:T(8,128)} %forward_images.1.value.mine, f32[32,256,128]{2,1,0:T(8,128)} %swap_images.1.other), custom_call_target="tpu_custom_call" | custom-call | tf_op jit(solution)/shard_map/back_project/pallas_call | solution.py:155
  48.3 33.8 %collect_gram.1 = (f32[256,256]{1,0:T(8,128)}, f32[2,8,16,256]{3,2,1,0:T(8,128)}) custom-call(f32[5,256,256]{2,1,0:T(8,128)} %back_project.1.bucket, bf16[1,256,256]{2,1,0:T(8,128)(2,1)} %probes.3), custom_call_target="tpu_custom_call" | custom-call | tf_op jit(solution)/shard_map/collect_gram/pallas_call | solution.py:251
  82.1 24.1 %factor_solve.1 = (f32[1,256,256]{2,1,0:T(8,128)}, f32[256,256]{1,0:T(8,128)}) custom-call(f32[256,256]{1,0:T(8,128)} %bitcast.1, f32[256,256]{1,0:T(8,128)} %get-tuple-element.5.field), custom_call_target="tpu_custom_call" | custom-call | tf_op jit(solution)/shard_map/factor_solve/pallas_call | solution.py:330

commit v2 on v1

--- a/solution.py
+++ b/solution.py
@@ -10,6 +10,7 @@
 
 MESH = pl.DeviceIdType.MESH
 REACH = 5
+LEVELS = 32766.0
 VMEM = pl.BlockSpec(memory_space=pltpu.VMEM)
 ANY = pl.BlockSpec(memory_space=pl.ANY)
 HIGHEST = lax.Precision.HIGHEST
@@ -170,7 +171,7 @@
     )(foot, live, jacobian, noise, mine, other)
 
 
-def collect_kernel(bands, split, bucket, probes, field, gram, got, relay, half, mine, parts, full, whole,
+def collect_kernel(bands, split, bucket, probes, field, gram, out_code, out_step, in_code, in_step, half, mine, parts, full, whole,
                    send, recv, gsend, grecv, asend, arecv):
     me, odd, mate, up, down = ring(bands)
     core = lax.axis_index("col")
@@ -179,26 +180,39 @@
     greet(peers + [partner])
     straight = {"tile": lax.rem(me + bands - 2 + 4 * odd, bands)}
     turned = {"tile": lax.rem(me + 2 + (bands - 4) * odd, bands)}
+    places = [{"tile": mate}, straight, {"tile": mate}, turned]
     hops = [
-        remote(bucket.at[1 + 2 * odd], got.at[0], send.at[0], recv.at[0], {"tile": mate}),
-        remote(bucket.at[4 * odd], got.at[2], send.at[1], recv.at[1], straight),
-        remote(bucket.at[3 - 2 * odd], got.at[1], send.at[2], recv.at[2], {"tile": mate}),
-        remote(relay, got.at[3], send.at[3], recv.at[3], turned),
+        (
+            remote(out_code.at[i], in_code.at[i], send.at[2 * i], recv.at[2 * i], place),
+            remote(out_step.at[i], in_step.at[i], send.at[2 * i + 1], recv.at[2 * i + 1], place),
+        )
+        for i, place in enumerate(places)
     ]
-    for hop in hops[:3]:
-        hop.start()
+
+    def launch(i, term):
+        top = jnp.maximum(jnp.max(jnp.abs(term), axis=0, keepdims=True), 1e-30)
+        code = jnp.round(term * (LEVELS / top))
+        out_code[i] = code.astype(jnp.int32).astype(jnp.int16)
+        out_step[i] = jnp.broadcast_to(top * (1.0 / LEVELS), out_step.shape[1:])
+        for hop in hops[i]:
+            hop.start()
+
+    def arrive(i):
+        for hop in hops[i]:
+            hop.wait_recv()
+        return in_code[i].astype(jnp.int32).astype(jnp.float32) * in_step[i][:1, :]
+
+    launch(0, bucket[1 + 2 * odd])
+    launch(1, bucket[4 * odd])
+    launch(2, bucket[3 - 2 * odd])
     base = probes[0].astype(jnp.float32).T + bucket[2]
-    hops[0].wait_recv()
-    relay[...] = bucket[4 - 4 * odd] + got[0]
-    hops[3].start()
-    hops[2].wait_recv()
-    base = base + got[1]
-    hops[1].wait_recv()
-    base = base + got[2]
-    hops[3].wait_recv()
-    field[...] = base + got[3]
-    for hop in hops:
-        hop.wait_send()
+    launch(3, bucket[4 - 4 * odd] + arrive(0))
+    base = base + arrive(2)
+    base = base + arrive(1)
+    field[...] = base + arrive(3)
+    for pair in hops:
+        for hop in pair:
+            hop.wait_send()
     value = field[...]
     local = lax.dot_general(
         value, value, (((1,), (1,)), ((), ())), precision=HIGHEST, preferred_element_type=jnp.float32
@@ -257,15 +271,17 @@
         in_specs=[VMEM, VMEM],
         out_specs=(VMEM, VMEM),
         scratch_shapes=[
-            pltpu.VMEM((4, width, cells), jnp.float32),
-            pltpu.VMEM((width, cells), jnp.float32),
+            pltpu.VMEM((4, width, cells), jnp.int16),
+            pltpu.VMEM((4, 8, cells), jnp.float32),
+            pltpu.VMEM((4, width, cells), jnp.int16),
+            pltpu.VMEM((4, 8, cells), jnp.float32),
             pltpu.VMEM((1, rows, width), jnp.float32),
             pltpu.VMEM((bands, piece, width), jnp.float32),
             pltpu.VMEM((bands - 1, piece, width), jnp.float32),
             pltpu.VMEM((bands, piece, width), jnp.float32),
             pltpu.VMEM((2, rows, width), jnp.float32),
-            pltpu.SemaphoreType.DMA((4,)),
-            pltpu.SemaphoreType.DMA((4,)),
+            pltpu.SemaphoreType.DMA((8,)),
+            pltpu.SemaphoreType.DMA((8,)),
             pltpu.SemaphoreType.DMA((bands,)),
             pltpu.SemaphoreType.DMA((bands,)),
             pltpu.SemaphoreType.DMA((bands,)),
@@ -277,27 +293,37 @@
     return field, gram.reshape(width, width)
 
 
-def eliminate(block):
-    size = block.shape[0]
-    groups = [block[8 * g : 8 * g + 8] for g in range(size // 8)]
-    sub = lax.broadcasted_iota(jnp.int32, (8, 1), 0)
-    for g in range(len(groups)):
+def eliminate(pieces):
+    size = pieces[0].shape[0]
+    lanes = pieces[0].shape[1]
+    count = size // 8
+    groups = [[piece[8 * g : 8 * g + 8] for piece in pieces] for g in range(count)]
+    sub = lax.broadcasted_iota(jnp.int32, (8, lanes), 0)
+    for g in range(count):
         panel = groups[g]
-        scaled = []
+        pivots = jnp.ones((8, lanes), jnp.float32)
         for i in range(8):
             j = 8 * g + i
-            r = lax.rsqrt(panel[i : i + 1, j : j + 1])
-            upper = panel[i : i + 1, :] * r
-            factor = jnp.where(sub > i, panel[:, j : j + 1] * r, 0.0)
-            panel = jnp.where(sub == i, upper, panel - factor * upper)
-            scaled.append((j, r, upper))
+            column = jnp.broadcast_to(panel[0][:, j : j + 1], (8, lanes))
+            pivot = jnp.broadcast_to(column[i : i + 1, :], (8, lanes))
+            ratio = jnp.where(sub > i, column / pivot, 0.0)
+            pivots = jnp.where(sub == i, pivot, pivots)
+            panel = [part - ratio * part[i : i + 1, :] for part in panel]
+        root = lax.rsqrt(pivots)
+        panel = [part * root for part in panel]
         groups[g] = panel
-        for h in range(g + 1, len(groups)):
+        if g + 1 == count:
+            break
+        turned = panel[0].T
+        for h in range(g + 1, count):
             rest = groups[h]
-            for j, r, upper in scaled:
-                rest = rest - (rest[:, j : j + 1] * r) * upper
+            for i in range(8):
+                lower = jnp.broadcast_to(turned[8 * h : 8 * h + 8, i : i + 1], (8, lanes))
+                rest = [r - lower * u[i : i + 1, :] for r, u in zip(rest, panel)]
             groups[h] = rest
-    return jnp.concatenate(groups, axis=0)
+    return [
+        jnp.concatenate([group[k] for group in groups], axis=0) for k in range(len(pieces))
+    ]
 
 
 def finish_kernel(scale, gram, field, basis, factor, inverse):
@@ -308,18 +334,18 @@
     unit = jnp.where(row == lane, 1.0, 0.0).astype(jnp.float32)
     keep = lane >= row
     zeros = jnp.zeros((half, half), jnp.float32)
-    top = eliminate(jnp.concatenate([gram[:half, :], unit], axis=1))
-    side = top[:, half:width]
-    inverse[:half, :half] = top[:, width:]
+    corner, side, start = eliminate([gram[:half, :half], gram[:half, half:], unit])
+    inverse[:half, :half] = start
     inverse[:half, half:] = zeros
-    factor[:half, :half] = jnp.where(keep, top[:, :half], 0.0) * (1.0 / scale)
+    factor[:half, :half] = jnp.where(keep, corner, 0.0) * (1.0 / scale)
     factor[:half, half:] = side * (1.0 / scale)
-    change = jnp.dot(side.T, top[:, half:], precision=HIGHEST, preferred_element_type=jnp.float32)
-    low = eliminate(
-        jnp.concatenate([gram[half:, half:] - change[:, :half], -change[:, half:], unit], axis=1)
-    )
-    inverse[half:, :] = low[:, half:]
-    factor[half:, half:] = jnp.where(keep, low[:, :half], 0.0) * (1.0 / scale)
+    across = side.T
+    change = jnp.dot(across, side, precision=HIGHEST, preferred_element_type=jnp.float32)
+    carry = jnp.dot(across, start, precision=HIGHEST, preferred_element_type=jnp.float32)
+    last, below, end = eliminate([gram[half:, half:] - change, -carry, unit])
+    inverse[half:, :half] = below
+    inverse[half:, half:] = end
+    factor[half:, half:] = jnp.where(keep, last, 0.0) * (1.0 / scale)
     factor[half:, :half] = zeros
     solved = jnp.dot(inverse[...], field[...], precision=HIGHEST, preferred_element_type=jnp.float32)
     basis[0] = (solved * scale).T

time: 107 us -> 114 us (1.065)
  Pallas kernels: 103 us -> 111 us
    pallas_call x1, Pallas kernels: 24.1 us -> 36 us  [finish(): pl.pallas_call(functools.partial(finish_kernel, scale), out_shape=(jax.Sh...]
    pallas_call x1, Pallas kernels: 33.8 us -> 29.5 us  [collect(): pl.pallas_call(functools.partial(collect_kernel, bands, split), out_shape...]
where the time goes in v2:
time: 114 us
  Pallas kernels  111 us (97%)
  local copies, waits for them, and re-layouts  1.38 us (1%)
  between operations  1.3 us (1%)
    pallas_call x1, Pallas kernels, finish(): pl.pallas_call(functools.partial(finish_kernel, scale), out_shape=(jax.Sh...  36 us
    pallas_call x1, Pallas kernels, collect(): pl.pallas_call(functools.partial(collect_kernel, bands, split), out_shape...  29.5 us
    pallas_call x1, Pallas kernels, fetch_window(): pl.pallas_call(functools.partial(window_kernel, bands), out_shape=jax.Sha...  16.9 us
    pallas_call x1, Pallas kernels, backward(): pl.pallas_call(functools.partial(backward_kernel, group, reach), out_shap...  11.1 us
    pallas_call x1, Pallas kernels, forward(): pl.pallas_call(functools.partial(forward_kernel, group, reach), out_shape...  10.1 us
    pallas_call x1, Pallas kernels, swap_cores(): pl.pallas_call(swap_kernel, out_shape=jax.ShapeDtypeStruct(value.shape, v...  7.52 us

profile of v2, /device:TPU:0, one launch (start us, length us, event | category | flops | bytes accessed | tf_op | source)
XLA Modules:
  0.0 113.7 jit_solution(2260161230560772192)
XLA Ops:
  1.3 0.8 copy.8
  2.0 0.6 reshape.10.foot
  2.7 16.9 %fetch_window.1.window = bf16[5,256,256]{2,1,0:T(8,128)(2,1)} custom-call(bf16[1,256,256]{2,1,0:T(8,128)(2,1)} %probes.3), custom_call_target="tpu_custom_call" | custom-call | tf_op jit(solution)/shard_map/fetch_window/pallas_call | solution.py:66
  19.6 10.1 %forward_images.1.value.mine = f32[32,256,128]{2,1,0:T(8,128)} custom-call(s32[96]{0:T(128)} %reshape.10.foot, bf16[32,3,128,256]{3,2,1,0:T(8,128)(2,1)} %jac.3, bf16[5,256,256]{2,1,0:T(8,128)(2,1)} %fetch_window.1.window), custom_call_target="tpu_custom_call" | custom-call | tf_op jit(solution)/shard_map/forward_images/pallas_call | solution.py:99
  29.7 7.5 %swap_images.1.other = f32[32,256,128]{2,1,0:T(8,128)} custom-call(f32[32,256,128]{2,1,0:T(8,128)} %forward_images.1.value.mine), custom_call_target="tpu_custom_call" | custom-call | tf_op jit(solution)/shard_map/swap_images/pallas_call | solution.py:125
  37.2 11.1 %back_project.1.bucket = f32[5,256,256]{2,1,0:T(8,128)} custom-call(s32[96]{0:T(128)} %reshape.10.foot, s32[1]{0:T(128)S(6)} %copy.9.live, bf16[32,3,128,256]{3,2,1,0:T(8,128)(2,1)} %jac.3, f32[32,128]{1,0:T(8,128)} %noise.1, f32[32,256,128]{2,1,0:T(8,128)} %forward_images.1.value.mine, f32[32,256,128]{2,1,0:T(8,128)} %swap_images.1.other), custom_call_target="tpu_custom_call" | custom-call | tf_op jit(solution)/shard_map/back_project/pallas_call | solution.py:156
  48.3 29.5 %collect_gram.1 = (f32[256,256]{1,0:T(8,128)}, f32[2,8,16,256]{3,2,1,0:T(8,128)}) custom-call(f32[5,256,256]{2,1,0:T(8,128)} %back_project.1.bucket, bf16[1,256,256]{2,1,0:T(8,128)(2,1)} %probes.3), custom_call_target="tpu_custom_call" | custom-call | tf_op jit(solution)/shard_map/collect_gram/pallas_call | solution.py:265
  77.8 36.0 %factor_solve.1 = (f32[1,256,256]{2,1,0:T(8,128)}, f32[256,256]{1,0:T(8,128)}) custom-call(f32[256,256]{1,0:T(8,128)} %bitcast.1, f32[256,256]{1,0:T(8,128)} %get-tuple-element.5.field), custom_call_target="tpu_custom_call" | custom-call | tf_op jit(solution)/shard_map/factor_solve/pallas_call | solution.py:356

commit v3 on v1

--- a/solution.py
+++ b/solution.py
@@ -10,6 +10,8 @@
 
 MESH = pl.DeviceIdType.MESH
 REACH = 5
+LEVELS = 32766.0
+PARTS = 2
 VMEM = pl.BlockSpec(memory_space=pltpu.VMEM)
 ANY = pl.BlockSpec(memory_space=pl.ANY)
 HIGHEST = lax.Precision.HIGHEST
@@ -38,139 +40,158 @@
     return me, odd, mate, up, down
 
 
-def window_kernel(bands, probes, window, send, recv):
+def images_kernel(bands, group, reach, foot, live, noise, probes, jac, out, held, window, turned,
+                  mine, other, load, send, recv, csend, crecv):
     me, odd, mate, up, down = ring(bands)
-    greet([{"tile": mate}, {"tile": up}, {"tile": down}])
-    own = probes.at[0]
-    hops = [
-        remote(own, window.at[0], send.at[0], recv.at[0], {"tile": up}),
-        remote(own, window.at[4], send.at[1], recv.at[1], {"tile": down}),
-        remote(own, window.at[1 + 2 * odd], send.at[2], recv.at[2], {"tile": mate}),
-        remote(window.at[4 - 4 * odd], window.at[3 - 2 * odd], send.at[3], recv.at[3], {"tile": mate}),
-    ]
-    for hop in hops[:3]:
-        hop.start()
+    partner = {"col": 1 - lax.axis_index("col")}
+    slots = jac.shape[0]
+    chunks = slots // group
+    cells = window.shape[1]
+    part = cells // PARTS
+
+    def fetch(c):
+        span = pl.ds(c * group, group)
+        return pltpu.make_async_copy(jac.at[span], held.at[span], load.at[c])
+
+    def swap(c):
+        span = pl.ds(c * group, group)
+        return remote(mine.at[span], other.at[span], csend.at[c], crecv.at[c], partner)
+
+    def turn(o):
+        turned[o] = window[o].astype(jnp.float32).T.astype(turned.dtype)
+
+    for c in range(chunks):
+        fetch(c).start()
+    greet([{"tile": mate}, {"tile": up}, {"tile": down}, partner])
+    hops = []
+    for h in range(PARTS):
+        span = pl.ds(h * part, part)
+        own = probes.at[0, span]
+        hops.append([
+            remote(own, window.at[0, span], send.at[h, 0], recv.at[h, 0], {"tile": up}),
+            remote(own, window.at[4, span], send.at[h, 1], recv.at[h, 1], {"tile": down}),
+            remote(own, window.at[1 + 2 * odd, span], send.at[h, 2], recv.at[h, 2], {"tile": mate}),
+            remote(window.at[4 - 4 * odd, span], window.at[3 - 2 * odd, span],
+                   send.at[h, 3], recv.at[h, 3], {"tile": mate}),
+        ])
+    for hop in hops:
+        for i in range(3):
+            hop[i].start()
     window[2] = probes[0]
-    hops[0].wait_recv()
-    hops[1].wait_recv()
-    hops[3].start()
-    hops[2].wait_recv()
-    hops[3].wait_recv()
-    for hop in hops:
-        hop.wait_send()
-
-
-def fetch_window(probes, bands):
-    _, cells, width = probes.shape
+    turn(2)
+    for h in range(PARTS):
+        span = pl.ds(h * part, part)
+        remote(probes.at[0, span], window.at[4 - 4 * odd, span], send.at[h, 0],
+               recv.at[h, 1 - odd], {"tile": up}).wait_recv()
+        hops[h][3].start()
+    for h in range(PARTS):
+        span = pl.ds(h * part, part)
+        hops[h][2].wait_recv()
+        remote(probes.at[0, span], window.at[4 * odd, span], send.at[h, 0],
+               recv.at[h, odd], {"tile": up}).wait_recv()
+    turn(4)
+    turn(0)
+    for h in range(PARTS):
+        hops[h][3].wait_recv()
+    turn(1)
+    turn(3)
+
+    def step(c, carry):
+        fetch(c).wait()
+        for g in range(group):
+            slot = c * group + g
+            total = None
+            for f in range(reach):
+                o = foot[slot * reach + f]
+                term = lax.dot_general(
+                    turned[o], held[slot, f], (((1,), (1,)), ((), ())),
+                    preferred_element_type=jnp.float32,
+                )
+                total = term if total is None else total + term
+            mine[slot] = total
+        swap(c).start()
+        return carry
+
+    lax.fori_loop(0, chunks, step, 0)
+
+    def close(c, carry):
+        swap(c).wait_recv()
+        for g in range(group):
+            slot = c * group + g
+            active = jnp.where(slot < live[0], 1.0, 0.0).astype(jnp.float32)
+            scale = noise[pl.ds(slot, 1), :] * active
+            out[slot] = ((mine[slot] + other[slot]) * scale).astype(out.dtype)
+        swap(c).wait_send()
+        return carry
+
+    lax.fori_loop(0, chunks, close, 0)
+    for hop in hops:
+        for i in range(4):
+            hop[i].wait_send()
+
+
+def images(foot, live, noise, probes, jacobian, bands, group):
+    slots, reach, rows, cells = jacobian.shape
+    width = probes.shape[2]
+    smem = pl.BlockSpec(memory_space=pltpu.SMEM)
+    chunks = slots // group
     return pl.pallas_call(
-        functools.partial(window_kernel, bands),
-        out_shape=jax.ShapeDtypeStruct((REACH, cells, width), probes.dtype),
-        in_specs=[VMEM],
+        functools.partial(images_kernel, bands, group, reach),
+        out_shape=jax.ShapeDtypeStruct((slots, width, rows), jnp.bfloat16),
+        in_specs=[smem, smem, VMEM, VMEM, ANY],
         out_specs=VMEM,
-        scratch_shapes=[pltpu.SemaphoreType.DMA((4,)), pltpu.SemaphoreType.DMA((4,))],
-        compiler_params=pltpu.CompilerParams(collective_id=0, has_side_effects=True),
-        name="fetch_window",
-    )(probes)
-
-
-def forward_kernel(group, reach, foot, jac, window, out, turned):
+        scratch_shapes=[
+            pltpu.VMEM(jacobian.shape, jacobian.dtype),
+            pltpu.VMEM((REACH, cells, width), probes.dtype),
+            pltpu.VMEM((REACH, width, cells), probes.dtype),
+            pltpu.VMEM((slots, width, rows), jnp.float32),
+            pltpu.VMEM((slots, width, rows), jnp.float32),
+            pltpu.SemaphoreType.DMA((chunks,)),
+            pltpu.SemaphoreType.DMA((PARTS, 4)),
+            pltpu.SemaphoreType.DMA((PARTS, 4)),
+            pltpu.SemaphoreType.DMA((chunks,)),
+            pltpu.SemaphoreType.DMA((chunks,)),
+        ],
+        compiler_params=pltpu.CompilerParams(
+            collective_id=0, has_side_effects=True, vmem_limit_bytes=48 * 1024 * 1024
+        ),
+        name="weighted_images",
+    )(foot, live, noise, probes, jacobian)
+
+
+def backward_kernel(group, reach, foot, jac, weighted, bucket):
     step = pl.program_id(0)
 
     @pl.when(step == 0)
     def _():
-        for o in range(REACH):
-            turned[o] = window[o].astype(jnp.float32).T.astype(turned.dtype)
+        bucket[...] = jnp.zeros_like(bucket)
 
     for g in range(group):
-        total = None
         for f in range(reach):
             o = foot[(step * group + g) * reach + f]
-            part = lax.dot_general(
-                turned[o], jac[g, f], (((1,), (1,)), ((), ())), preferred_element_type=jnp.float32
-            )
-            total = part if total is None else total + part
-        out[g] = total
-
-
-def forward(foot, jacobian, window, group):
+            bucket[o] += jnp.dot(weighted[g], jac[g, f], preferred_element_type=jnp.float32)
+
+
+def backward(foot, jacobian, weighted, group):
     slots, reach, rows, cells = jacobian.shape
-    width = window.shape[2]
+    width = weighted.shape[1]
     return pl.pallas_call(
-        functools.partial(forward_kernel, group, reach),
-        out_shape=jax.ShapeDtypeStruct((slots, width, rows), jnp.float32),
+        functools.partial(backward_kernel, group, reach),
+        out_shape=jax.ShapeDtypeStruct((REACH, width, cells), jnp.float32),
         grid_spec=pltpu.PrefetchScalarGridSpec(
             num_scalar_prefetch=1,
             grid=(slots // group,),
             in_specs=[
                 pl.BlockSpec((group, reach, rows, cells), lambda i, foot: (i, 0, 0, 0)),
-                pl.BlockSpec((REACH, cells, width), lambda i, foot: (0, 0, 0)),
+                pl.BlockSpec((group, width, rows), lambda i, foot: (i, 0, 0)),
             ],
-            out_specs=pl.BlockSpec((group, width, rows), lambda i, foot: (i, 0, 0)),
-            scratch_shapes=[pltpu.VMEM((REACH, width, cells), window.dtype)],
-        ),
-        name="forward_images",
-    )(foot, jacobian, window)
-
-
-def swap_kernel(value, other, send, recv):
-    partner = {"col": 1 - lax.axis_index("col")}
-    greet([partner])
-    hop = remote(value, other, send, recv, partner)
-    hop.start()
-    hop.wait()
-
-
-def swap_cores(value):
-    return pl.pallas_call(
-        swap_kernel,
-        out_shape=jax.ShapeDtypeStruct(value.shape, value.dtype),
-        in_specs=[ANY],
-        out_specs=ANY,
-        scratch_shapes=[pltpu.SemaphoreType.DMA, pltpu.SemaphoreType.DMA],
-        compiler_params=pltpu.CompilerParams(collective_id=1, has_side_effects=True),
-        name="swap_images",
-    )(value)
-
-
-def backward_kernel(group, reach, foot, live, jac, noise, mine, other, bucket):
-    step = pl.program_id(0)
-
-    @pl.when(step == 0)
-    def _():
-        bucket[...] = jnp.zeros_like(bucket)
-
-    for g in range(group):
-        slot = step * group + g
-        active = jnp.where(slot < live[0], 1.0, 0.0).astype(jnp.float32)
-        scale = noise[pl.ds(slot, 1), :] * active
-        weighted = ((mine[g] + other[g]) * scale).astype(jnp.bfloat16)
-        for f in range(reach):
-            o = foot[slot * reach + f]
-            bucket[o] += jnp.dot(weighted, jac[g, f], preferred_element_type=jnp.float32)
-
-
-def backward(foot, live, jacobian, noise, mine, other, group):
-    slots, reach, rows, cells = jacobian.shape
-    width = mine.shape[1]
-    return pl.pallas_call(
-        functools.partial(backward_kernel, group, reach),
-        out_shape=jax.ShapeDtypeStruct((REACH, width, cells), jnp.float32),
-        grid_spec=pltpu.PrefetchScalarGridSpec(
-            num_scalar_prefetch=2,
-            grid=(slots // group,),
-            in_specs=[
-                pl.BlockSpec((group, reach, rows, cells), lambda i, foot, live: (i, 0, 0, 0)),
-                pl.BlockSpec((slots, rows), lambda i, foot, live: (0, 0)),
-                pl.BlockSpec((group, width, rows), lambda i, foot, live: (i, 0, 0)),
-                pl.BlockSpec((group, width, rows), lambda i, foot, live: (i, 0, 0)),
-            ],
-            out_specs=pl.BlockSpec((REACH, width, cells), lambda i, foot, live: (0, 0, 0)),
+            out_specs=pl.BlockSpec((REACH, width, cells), lambda i, foot: (0, 0, 0)),
         ),
         name="back_project",
-    )(foot, live, jacobian, noise, mine, other)
-
-
-def collect_kernel(bands, split, bucket, probes, field, gram, got, relay, half, mine, parts, full, whole,
+    )(foot, jacobian, weighted)
+
+
+def collect_kernel(bands, split, bucket, probes, field, gram, out_code, out_step, in_code, in_step, half, mine, parts, full, whole,
                    send, recv, gsend, grecv, asend, arecv):
     me, odd, mate, up, down = ring(bands)
     core = lax.axis_index("col")
@@ -179,26 +200,39 @@
     greet(peers + [partner])
     straight = {"tile": lax.rem(me + bands - 2 + 4 * odd, bands)}
     turned = {"tile": lax.rem(me + 2 + (bands - 4) * odd, bands)}
+    places = [{"tile": mate}, straight, {"tile": mate}, turned]
     hops = [
-        remote(bucket.at[1 + 2 * odd], got.at[0], send.at[0], recv.at[0], {"tile": mate}),
-        remote(bucket.at[4 * odd], got.at[2], send.at[1], recv.at[1], straight),
-        remote(bucket.at[3 - 2 * odd], got.at[1], send.at[2], recv.at[2], {"tile": mate}),
-        remote(relay, got.at[3], send.at[3], recv.at[3], turned),
+        (
+            remote(out_code.at[i], in_code.at[i], send.at[2 * i], recv.at[2 * i], place),
+            remote(out_step.at[i], in_step.at[i], send.at[2 * i + 1], recv.at[2 * i + 1], place),
+        )
+        for i, place in enumerate(places)
     ]
-    for hop in hops[:3]:
-        hop.start()
+
+    def launch(i, term):
+        top = jnp.maximum(jnp.max(jnp.abs(term), axis=0, keepdims=True), 1e-30)
+        code = jnp.round(term * (LEVELS / top))
+        out_code[i] = code.astype(jnp.int32).astype(jnp.int16)
+        out_step[i] = jnp.broadcast_to(top * (1.0 / LEVELS), out_step.shape[1:])
+        for hop in hops[i]:
+            hop.start()
+
+    def arrive(i):
+        for hop in hops[i]:
+            hop.wait_recv()
+        return in_code[i].astype(jnp.int32).astype(jnp.float32) * in_step[i][:1, :]
+
+    launch(0, bucket[1 + 2 * odd])
+    launch(1, bucket[4 * odd])
+    launch(2, bucket[3 - 2 * odd])
     base = probes[0].astype(jnp.float32).T + bucket[2]
-    hops[0].wait_recv()
-    relay[...] = bucket[4 - 4 * odd] + got[0]
-    hops[3].start()
-    hops[2].wait_recv()
-    base = base + got[1]
-    hops[1].wait_recv()
-    base = base + got[2]
-    hops[3].wait_recv()
-    field[...] = base + got[3]
-    for hop in hops:
-        hop.wait_send()
+    launch(3, bucket[4 - 4 * odd] + arrive(0))
+    base = base + arrive(2)
+    base = base + arrive(1)
+    field[...] = base + arrive(3)
+    for pair in hops:
+        for hop in pair:
+            hop.wait_send()
     value = field[...]
     local = lax.dot_general(
         value, value, (((1,), (1,)), ((), ())), precision=HIGHEST, preferred_element_type=jnp.float32
@@ -257,15 +291,17 @@
         in_specs=[VMEM, VMEM],
         out_specs=(VMEM, VMEM),
         scratch_shapes=[
-            pltpu.VMEM((4, width, cells), jnp.float32),
-            pltpu.VMEM((width, cells), jnp.float32),
+            pltpu.VMEM((4, width, cells), jnp.int16),
+            pltpu.VMEM((4, 8, cells), jnp.float32),
+            pltpu.VMEM((4, width, cells), jnp.int16),
+            pltpu.VMEM((4, 8, cells), jnp.float32),
             pltpu.VMEM((1, rows, width), jnp.float32),
             pltpu.VMEM((bands, piece, width), jnp.float32),
             pltpu.VMEM((bands - 1, piece, width), jnp.float32),
             pltpu.VMEM((bands, piece, width), jnp.float32),
             pltpu.VMEM((2, rows, width), jnp.float32),
-            pltpu.SemaphoreType.DMA((4,)),
-            pltpu.SemaphoreType.DMA((4,)),
+            pltpu.SemaphoreType.DMA((8,)),
+            pltpu.SemaphoreType.DMA((8,)),
             pltpu.SemaphoreType.DMA((bands,)),
             pltpu.SemaphoreType.DMA((bands,)),
             pltpu.SemaphoreType.DMA((bands,)),
@@ -347,10 +383,8 @@
     group = math.gcd(slots, 4)
     foot = footprint.reshape(-1)
     split = (width // 2) % (8 * bands) == 0
-    window = fetch_window(probes, bands)
-    mine = forward(foot, jacobian, window, group)
-    other = swap_cores(mine)
-    bucket = backward(foot, live, jacobian, noise_weight, mine, other, group)
+    weighted = images(foot, live, noise_weight, probes, jacobian, bands, group)
+    bucket = backward(foot, jacobian, weighted, group)
     field, gram = collect(bucket, probes, bands, split)
     if not split:
         gram = lax.psum(gram, ("tile", "col"))

time: 107 us -> 90.9 us (0.85)
  Pallas kernels: 103 us -> 85.4 us
  local copies, waits for them, and re-layouts: 1.38 us -> 3.81 us
    pallas_call x3 -> x1, Pallas kernels: 34.5 us -> 23.5 us  [images(): pl.pallas_call(functools.partial(images_kernel, bands, group, reach), out...]
    pallas_call x1, Pallas kernels: 33.8 us -> 27.9 us  [collect(): pl.pallas_call(functools.partial(collect_kernel, bands, split), out_shape...]
    unnamed x1 -> x9, local copies, waits for them, and re-layouts: 0.76 us -> 3.7 us
    pallas_call x1, Pallas kernels: 11.1 us -> 9.82 us  [backward(): pl.pallas_call(functools.partial(backward_kernel, group, reach), out_shap...]
where the time goes in v3:
time: 90.9 us; the launch traced here: 90.5 us
  Pallas kernels  85.4 us (94%)
  local copies, waits for them, and re-layouts  3.81 us (4%)
  between operations  1.32 us (1%)
    pallas_call x1, Pallas kernels, collect(): pl.pallas_call(functools.partial(collect_kernel, bands, split), out_shape...  27.9 us
    pallas_call x1, Pallas kernels, finish(): pl.pallas_call(functools.partial(finish_kernel, scale), out_shape=(jax.Sh...  24.1 us
    pallas_call x1, Pallas kernels, images(): pl.pallas_call(functools.partial(images_kernel, bands, group, reach), out...  23.5 us
    pallas_call x1, Pallas kernels, backward(): pl.pallas_call(functools.partial(backward_kernel, group, reach), out_shap...  9.82 us
    unnamed x9, local copies, waits for them, and re-layouts  3.7 us

profile of v3, /device:TPU:0, one launch (start us, length us, event | category | flops | bytes accessed | tf_op | source)
XLA Modules:
  0.0 90.5 jit_solution(9380785076414608036)
XLA Ops:
  1.3 0.8 copy.8
  2.0 0.1 reshape.10.foot
  2.1 0.0 copy-start.1
  2.2 0.9 copy-done.1
  3.1 0.0 copy-start.2
  3.1 0.7 copy-done.2
  3.8 0.0 copy-start.3
  3.8 23.5 %weighted_images.1.weighted = bf16[32,256,128]{2,1,0:T(8,128)(2,1)S(1)} custom-call(s32[96]{0:T(128)S(1)} %reshape.10.foot, s32[1]{0:T(128)S(6)} %copy.9.live, f32[32,128]{1,0:T(8,128)S(1)} %copy-done.2, bf16[1,256,256]{2,1,0:T(8,128)(2,1)S(1)} %copy-done.1, bf16[32,3,128,256]{3,2,1,0:T(8,128)(2,1)} %jac.3), custom_call_target="tpu_custom_call" | custom-call | tf_op jit(solution)/shard_map/weighted_images/pallas_call | solution.py:138
  27.3 0.0 copy-done.3
  27.3 0.0 copy-start
  27.3 1.3 %copy-done = bf16[32,256,128]{2,1,0:T(8,128)(2,1)} copy-done((bf16[32,256,128]{2,1,0:T(8,128)(2,1)}, bf16[32,256,128]{2,1,0:T(8,128)(2,1)S(1)}, u32[]{:S(2)}) %copy-start) | copy-done | bytes 2097176
  28.6 9.8 %back_project.1.bucket = f32[5,256,256]{2,1,0:T(8,128)} custom-call(s32[96]{0:T(128)} %copy-done.3, bf16[32,3,128,256]{3,2,1,0:T(8,128)(2,1)} %jac.3, bf16[32,256,128]{2,1,0:T(8,128)(2,1)} %copy-done), custom_call_target="tpu_custom_call" | custom-call | tf_op jit(solution)/shard_map/back_project/pallas_call | solution.py:178
  38.5 27.9 %collect_gram.1 = (f32[256,256]{1,0:T(8,128)}, f32[2,8,16,256]{3,2,1,0:T(8,128)}) custom-call(f32[5,256,256]{2,1,0:T(8,128)} %back_project.1.bucket, bf16[1,256,256]{2,1,0:T(8,128)(2,1)} %probes.3), custom_call_target="tpu_custom_call" | custom-call | tf_op jit(solution)/shard_map/collect_gram/pallas_call | solution.py:285
  66.4 24.1 %factor_solve.1 = (f32[1,256,256]{2,1,0:T(8,128)}, f32[256,256]{1,0:T(8,128)}) custom-call(f32[256,256]{1,0:T(8,128)} %bitcast.1, f32[256,256]{1,0:T(8,128)} %get-tuple-element.5.field), custom_call_target="tpu_custom_call" | custom-call | tf_op jit(solution)/shard_map/factor_solve/pallas_call | solution.py:366
Async XLA Ops:
  2.1 0.9 %copy-start.1 = (bf16[1,256,256]{2,1,0:T(8,128)(2,1)S(1)}, bf16[1,256,256]{2,1,0:T(8,128)(2,1)}, u32[]{:S(2)}) copy-start(bf16[1,256,256]{2,1,0:T(8,128)(2,1)} %probes.3) | copy-start | bytes 393220
  3.1 0.7 copy-start.2
  3.8 23.5 %copy-start.3 = (s32[96]{0:T(128)}, s32[96]{0:T(128)S(1)}, u32[]{:S(2)}) copy-start(s32[96]{0:T(128)S(1)} %reshape.10.foot) | copy-start | bytes 1156
  27.3 1.3 %copy-start = (bf16[32,256,128]{2,1,0:T(8,128)(2,1)}, bf16[32,256,128]{2,1,0:T(8,128)(2,1)S(1)}, u32[]{:S(2)}) copy-start(bf16[32,256,128]{2,1,0:T(8,128)(2,1)S(1)} %weighted_images.1.weighted) | copy-start | bytes 6291460

commit v4 on v3

--- a/solution.py
+++ b/solution.py
@@ -192,7 +192,7 @@
 
 
 def collect_kernel(bands, split, bucket, probes, field, gram, out_code, out_step, in_code, in_step, half, mine, parts, full, whole,
-                   send, recv, gsend, grecv, asend, arecv):
+                   send, recv, gsend, grecv, asend, arecv, fsend, frecv):
     me, odd, mate, up, down = ring(bands)
     core = lax.axis_index("col")
     partner = {"col": 1 - core}
@@ -267,14 +267,20 @@
         hops.append(remote(full.at[me], full.at[me], asend.at[d], arecv.at[d], {"tile": target}))
     for hop in hops:
         hop.start()
-    for hop in hops:
-        hop.wait_recv()
+    shares = [remote(full.at[me], gram.at[core, me], fsend.at[0], frecv.at[0], partner)]
+    shares[0].start()
+    for d in range(1, bands):
+        source = lax.rem(me + bands - d, bands)
+        hops[d - 1].wait_recv()
+        shares.append(
+            remote(full.at[source], gram.at[core, source], fsend.at[d], frecv.at[d], partner)
+        )
+        shares[d].start()
+    gram[core] = full[...]
     for hop in hops:
         hop.wait_send()
-    hop = remote(full, gram.at[core], asend.at[0], arecv.at[0], partner)
-    hop.start()
-    gram[core] = full[...]
-    hop.wait()
+    for share in shares:
+        share.wait()
 
 
 def collect(bucket, probes, bands, split):
@@ -306,6 +312,8 @@
             pltpu.SemaphoreType.DMA((bands,)),
             pltpu.SemaphoreType.DMA((bands,)),
             pltpu.SemaphoreType.DMA((bands,)),
+            pltpu.SemaphoreType.DMA((bands,)),
+            pltpu.SemaphoreType.DMA((bands,)),
         ],
         compiler_params=pltpu.CompilerParams(collective_id=2, has_side_effects=True),
         name="collect_gram",

time: 90.9 us -> 91 us (level)
  no operation moved by 1% of the time
where the time goes in v4:
time: 91 us; the launch traced here: 90.6 us
  Pallas kernels  85.5 us (94%)
  local copies, waits for them, and re-layouts  3.81 us (4%)
  between operations  1.32 us (1%)
    pallas_call x1, Pallas kernels, collect(): pl.pallas_call(functools.partial(collect_kernel, bands, split), out_shape...  28 us
    pallas_call x1, Pallas kernels, finish(): pl.pallas_call(functools.partial(finish_kernel, scale), out_shape=(jax.Sh...  24.1 us
    pallas_call x1, Pallas kernels, images(): pl.pallas_call(functools.partial(images_kernel, bands, group, reach), out...  23.5 us
    pallas_call x1, Pallas kernels, backward(): pl.pallas_call(functools.partial(backward_kernel, group, reach), out_shap...  9.82 us
    unnamed x9, local copies, waits for them, and re-layouts  3.7 us

profile of v4, /device:TPU:0, one launch (start us, length us, event | category | flops | bytes accessed | tf_op | source)
XLA Modules:
  0.0 90.6 jit_solution(5731765805424686878)
XLA Ops:
  1.3 0.8 copy.8
  2.0 0.1 reshape.10.foot
  2.1 0.0 copy-start.1
  2.2 0.9 copy-done.1
  3.1 0.0 copy-start.2
  3.1 0.7 copy-done.2
  3.8 0.0 copy-start.3
  3.8 23.5 %weighted_images.1.weighted = bf16[32,256,128]{2,1,0:T(8,128)(2,1)S(1)} custom-call(s32[96]{0:T(128)S(1)} %reshape.10.foot, s32[1]{0:T(128)S(6)} %copy.9.live, f32[32,128]{1,0:T(8,128)S(1)} %copy-done.2, bf16[1,256,256]{2,1,0:T(8,128)(2,1)S(1)} %copy-done.1, bf16[32,3,128,256]{3,2,1,0:T(8,128)(2,1)} %jac.3), custom_call_target="tpu_custom_call" | custom-call | tf_op jit(solution)/shard_map/weighted_images/pallas_call | solution.py:138
  27.3 0.0 copy-done.3
  27.3 0.0 copy-start
  27.3 1.3 %copy-done = bf16[32,256,128]{2,1,0:T(8,128)(2,1)} copy-done((bf16[32,256,128]{2,1,0:T(8,128)(2,1)}, bf16[32,256,128]{2,1,0:T(8,128)(2,1)S(1)}, u32[]{:S(2)}) %copy-start) | copy-done | bytes 2097176
  28.6 9.8 %back_project.1.bucket = f32[5,256,256]{2,1,0:T(8,128)} custom-call(s32[96]{0:T(128)} %copy-done.3, bf16[32,3,128,256]{3,2,1,0:T(8,128)(2,1)} %jac.3, bf16[32,256,128]{2,1,0:T(8,128)(2,1)} %copy-done), custom_call_target="tpu_custom_call" | custom-call | tf_op jit(solution)/shard_map/back_project/pallas_call | solution.py:178
  38.5 28.0 %collect_gram.1 = (f32[256,256]{1,0:T(8,128)}, f32[2,8,16,256]{3,2,1,0:T(8,128)}) custom-call(f32[5,256,256]{2,1,0:T(8,128)} %back_project.1.bucket, bf16[1,256,256]{2,1,0:T(8,128)(2,1)} %probes.3), custom_call_target="tpu_custom_call" | custom-call | tf_op jit(solution)/shard_map/collect_gram/pallas_call | solution.py:291
  66.5 24.1 %factor_solve.1 = (f32[1,256,256]{2,1,0:T(8,128)}, f32[256,256]{1,0:T(8,128)}) custom-call(f32[256,256]{1,0:T(8,128)} %bitcast.1, f32[256,256]{1,0:T(8,128)} %get-tuple-element.5.field), custom_call_target="tpu_custom_call" | custom-call | tf_op jit(solution)/shard_map/factor_solve/pallas_call | solution.py:374
Async XLA Ops:
  2.1 0.9 %copy-start.1 = (bf16[1,256,256]{2,1,0:T(8,128)(2,1)S(1)}, bf16[1,256,256]{2,1,0:T(8,128)(2,1)}, u32[]{:S(2)}) copy-start(bf16[1,256,256]{2,1,0:T(8,128)(2,1)} %probes.3) | copy-start | bytes 393220
  3.1 0.7 copy-start.2
  3.8 23.5 %copy-start.3 = (s32[96]{0:T(128)}, s32[96]{0:T(128)S(1)}, u32[]{:S(2)}) copy-start(s32[96]{0:T(128)S(1)} %reshape.10.foot) | copy-start | bytes 1156
  27.3 1.3 %copy-start = (bf16[32,256,128]{2,1,0:T(8,128)(2,1)}, bf16[32,256,128]{2,1,0:T(8,128)(2,1)S(1)}, u32[]{:S(2)}) copy-start(bf16[32,256,128]{2,1,0:T(8,128)(2,1)S(1)} %weighted_images.1.weighted) | copy-start | bytes 6291460
